TPU v7x, 32 devices: a whole 2x2x4 slice. The times are simulated.
32 devices in a mesh: pts: 16 (over z, x, core), modes: 2 (over y).
Axes of the slice: x: 2, y: 2, z: 4, core: 2. Of those that a mesh axis runs over, the one named last changes fastest.
Arguments:
- features: bfloat16 [65536, 128], P('pts'), may hold values from -6 to 6
- coords: float32 [3, 65536], P(None, 'pts'), may hold values from 0 to 1
- quad_weight: float32 [65536], P('pts'), may hold values from 0.5 to 6, as said below
- mode_table: int32 [3, 8192], replicated, may hold values from -8 to 31, as said below
- mode_weight: bfloat16 [8192, 2, 128, 128], P(('pts', 'modes')), may hold values from -4 to 4
- lin_weight: bfloat16 [128, 128], replicated, may hold values from -0.5 to 0.5
- bias: float32 [128], replicated, may hold values from -3 to 3
Outputs:
- output: bfloat16 [65536, 128], P(('pts', 'modes'))
Inputs may be any that keep to these rules, and one draw needn't show every extreme that they name: `mode_table`: each column is a distinct triple (kx, ky, kz) with -8 <= kx < 8, -8 <= ky < 8, 0 <= kz < 32; every such triple appears exactly once, in an order drawn from the seed. `quad_weight`: Positive.
All inputs are finite; a program needn't handle non-finite values.
Results may differ from a plain program's by a relative error of at most 0.018.
Values may be sent and summed in bfloat16 or wider, within the bound.
A program may use at most 128 MiB of HBM per device.

v0:
```python
import math
import jax
import jax.numpy as jnp
from jax import lax
from jax.sharding import PartitionSpec as P


def phase_basis(coords, wave):
    turns = coords[0][:, None] * wave[0][None, :] + coords[1][:, None] * wave[1][None, :]
    turns = turns + coords[2][:, None] * wave[2][None, :]
    angle = 2.0 * math.pi * turns
    return jnp.concatenate([jnp.cos(angle), -jnp.sin(angle)], axis=1).astype(jnp.bfloat16)


def on_device(features, coords, quad_weight, mode_table, mode_weight, lin_weight, bias):
    width = features.shape[1]
    local_pts = features.shape[0]
    own_modes = mode_weight.shape[0]
    n_pts = lax.axis_size("pts")
    n_groups = lax.axis_size("modes")
    group = lax.axis_index("modes")
    group_modes = n_pts * own_modes
    weighted = (quad_weight[:, None] * features.astype(jnp.float32)).astype(jnp.bfloat16)
    total = lax.psum(jnp.sum(quad_weight), "pts")
    wave_all = mode_table.astype(jnp.float32)
    grouped = wave_all.reshape(3, n_pts, n_groups, own_modes)
    wave_group = lax.dynamic_slice_in_dim(grouped, group, 1, 2).reshape(3, group_modes)
    basis_all = phase_basis(coords, wave_group)

    def pick_columns(rows):
        cosine = lax.slice_in_dim(basis_all, 0, rows, axis=1)
        sine = lax.dynamic_slice_in_dim(basis_all, group_modes, rows, 1)
        return jnp.concatenate([cosine, sine], axis=1)

    basis = pick_columns(lax.axis_size("pts") * own_modes)
    term = lax.dot_general(
        basis, weighted, (((0,), (0,)), ((), ())), preferred_element_type=jnp.float32
    )
    coef = lax.psum_scatter(
        term.reshape(2, lax.axis_size("pts") * own_modes, width)
        .transpose(1, 0, 2)
        .reshape(lax.axis_size("pts") * own_modes, 2 * width)
        .astype(jnp.bfloat16),
        "pts",
        scatter_dimension=0,
        tiled=True,
    )
    real_in = coef[:, :width]
    imag_in = coef[:, width:]
    w_real = mode_weight[:, 0]
    w_imag = mode_weight[:, 1]
    real_out = jnp.einsum(
        "mc,mcd->md", real_in, w_real, preferred_element_type=jnp.float32
    ) - jnp.einsum("mc,mcd->md", imag_in, w_imag, preferred_element_type=jnp.float32)
    imag_out = jnp.einsum(
        "mc,mcd->md", real_in, w_imag, preferred_element_type=jnp.float32
    ) + jnp.einsum("mc,mcd->md", imag_in, w_real, preferred_element_type=jnp.float32)
    filtered = jnp.concatenate([real_out, imag_out], axis=1).astype(jnp.bfloat16)
    out_rows = local_pts // n_groups
    my_features = lax.dynamic_slice_in_dim(features, group * out_rows, out_rows, 0)
    piece = lax.all_gather(filtered, "pts", axis=0, tiled=True)
    basis = pick_columns(piece.shape[0])
    rhs = jnp.concatenate([piece[:, :width], piece[:, width:]], axis=0)
    field = jnp.dot(basis, rhs, preferred_element_type=jnp.float32)
    spectral = lax.psum_scatter(
        field.astype(jnp.bfloat16), "modes", scatter_dimension=0, tiled=True
    ).astype(jnp.float32)
    linear = jnp.dot(my_features, lin_weight, preferred_element_type=jnp.float32)
    pre = spectral / total + linear + bias[None, :]
    return jax.nn.gelu(pre, approximate=False).astype(jnp.bfloat16)


def solution(mesh):
    return jax.shard_map(
        on_device,
        mesh=mesh,
        in_specs=(
            P("pts", None),
            P(None, "pts"),
            P("pts"),
            P(),
            P(("pts", "modes"), None, None, None),
            P(),
            P(),
        ),
        out_specs=P(("pts", "modes"), None),
        check_vma=False,
    )
```

profile of v0, /device:TPU:0, one launch (start us, length us, event | category | flops | bytes accessed | tf_op | source)
XLA Modules:
  0.0 505.3 jit_solution(14802626488108388729)
XLA Ops:
  6.5 0.9 convert_element_type.32
  7.5 0.1 reshape.19
  7.6 1.0 fusion.36
  8.6 0.1 constant_dynamic-slice_fusion.1
  8.7 264.3 %cosine_convert_fusion = (bf16[4096,4096]{1,0:T(8,128)(2,1)}, bf16[4096,4096]{1,0:T(8,128)(2,1)}) fusion(f32[4096]{0:T(1024)S(1)} %bitcast.45, f32[4096]{0:T(1024)S(1)} %bitcast.47, f32[4096]{0:T(1024)S(1)} %bitcast.44, f32[4096]{0:T(1024)S(1)} %bitcast.48, f32[4096]{0:T(1024)S(1)} %bitcast.43, f32[4096]{0:T(1024)S(1)} %bitcast.46), kind=kLoop, calls=%fused_computation.2 | loop fusion | flops 150994944 | bytes 67207168 | tf_op jit(solution)/shard_map/convert.2
  273.0 27.4 %fusion.2 = bf16[8192,128]{1,0:T(8,128)(2,1)S(1)} fusion(bf16[4096,4096]{1,0:T(8,128)(2,1)} %get-tuple-element.10, bf16[4096,4096]{1,0:T(8,128)(2,1)} %get-tuple-element.9, bf16[4096,128]{1,0:T(8,128)(2,1)S(1)} %copy-done.2, f32[4096]{0:T(1024)S(1)} %copy-done.1), kind=kOutput, calls=%fused_computation.6 | convolution fusion | flops 8726773760 | bytes 70270976 | tf_op jit(solution)/shard_map/dot_general | solution.py:36
  300.3 2.8 copy.8
  303.2 0.2 all-gather.2.cloned.1.call-start
  303.4 64.5 %reduce-scatter.3.cloned.1.call-done = bf16[256,256]{0,1:T(8,128)(2,1)} async-done(((bf16[4096,256]{0,1:T(8,128)(2,1)}), bf16[256,256]{0,1:T(8,128)(2,1)}) %reduce-scatter.3.cloned.1.call-update) | async-done | bytes 131088 | tf_op jit(solution)/shard_map/reduce_scatter | solution.py:39
  367.9 0.9 slice_bitcast_fusion
  368.8 0.1 copy.9
  368.9 5.7 %fusion.9 = f32[256,1,128]{2,1,0:T(1,128)S(1)} fusion(bf16[256,128,1]{1,2,0:T(2,128)(2,1)S(1)} %copy.9, bf16[256,2,128,128]{3,2,1,0:T(8,128)(2,1)} %param.11), kind=kOutput, calls=%fused_computation.13 | convolution fusion | flops 8388608 | bytes 8585216 | tf_op jit(solution)/shard_map/mc,mcd->md/dot_general | solution.py:52
  374.6 5.7 %fusion.3 = f32[256,1,128]{2,1,0:T(1,128)S(1)} fusion(bf16[256,128,1]{1,2,0:T(2,128)(2,1)S(1)} %copy.9, bf16[256,2,128,128]{3,2,1,0:T(8,128)(2,1)} %param.11), kind=kOutput, calls=%fused_computation.7 | convolution fusion | flops 8388608 | bytes 8585216 | tf_op jit(solution)/shard_map/mc,mcd->md/dot_general | solution.py:55
  380.3 0.1 copy.11
  380.4 5.7 %fusion.5 = f32[256,1,128]{2,1,0:T(1,128)S(1)} fusion(bf16[256,128,1]{1,2,0:T(2,128)(2,1)S(1)} %copy.11, bf16[256,2,128,128]{3,2,1,0:T(8,128)(2,1)} %param.11), kind=kOutput, calls=%fused_computation.9 | convolution fusion | flops 8388608 | bytes 8585216 | tf_op jit(solution)/shard_map/mc,mcd->md/dot_general | solution.py:54
  386.1 5.7 %fusion.7 = f32[256,1,128]{2,1,0:T(1,128)S(1)} fusion(bf16[256,128,1]{1,2,0:T(2,128)(2,1)S(1)} %copy.11, bf16[256,2,128,128]{3,2,1,0:T(8,128)(2,1)} %param.11), kind=kOutput, calls=%fused_computation.11 | convolution fusion | flops 8388608 | bytes 8585216 | tf_op jit(solution)/shard_map/mc,mcd->md/dot_general | solution.py:57
  391.9 0.7 pad_maximum_fusion.7
  392.6 0.0 reduce-scatter.5.cloned.1.call-start
  392.6 40.5 %all-gather.2.cloned.1.call-done = bf16[4096,256]{1,0:T(8,128)(2,1)} async-done(((bf16[256,256]{1,0:T(8,128)(2,1)}), bf16[4096,256]{1,0:T(8,128)(2,1)}) %all-gather.2.cloned.1.call-update) | async-done | bytes 2097168 | tf_op jit(solution)/shard_map/all_gather | solution.py:61
  433.1 1.7 fusion.35
  434.8 26.5 %fusion.15 = bf16[4096,128]{1,0:T(8,128)(2,1)} fusion(bf16[4096,4096]{1,0:T(8,128)(2,1)} %get-tuple-element.10, bf16[4096,4096]{1,0:T(8,128)(2,1)} %get-tuple-element.9, bf16[4096,128]{1,0:T(8,128)(2,1)S(1)} %get-tuple-element.6, bf16[4096,128]{1,0:T(8,128)(2,1)S(1)} %get-tuple-element.5), kind=kOutput, calls=%fused_computation.19 | convolution fusion | flops 8728870912 | bytes 70254592 | tf_op jit(solution)/shard_map/dot_general | solution.py:64
  461.3 0.6 reduce_sum.9
  461.9 32.0 %psum.7 = f32[]{:T(128)} all-reduce(f32[]{:T(128)} %reduce_sum.9), channel_id=1, replica_groups=mesh['pts'=16,'modes'=2] {'pts'}, use_global_device_ids=true, to_apply=%region_3.0 | all-reduce | flops 1 | bytes 8 | tf_op jit(solution)/shard_map/psum | solution.py:24
  493.9 4.9 fusion.22
  (14 shorter events, 0.1 us)
Async XLA Ops:
  6.5 487.3 %copy-start = (bf16[128,128]{1,0:T(8,128)(2,1)S(1)}, bf16[128,128]{1,0:T(8,128)(2,1)}, u32[]{:S(2)}) copy-start(bf16[128,128]{1,0:T(8,128)(2,1)} %param.12) | copy-start | bytes 98308
  6.5 361.4 %reduce-scatter.3.cloned.1.call-start = ((), (), s32[]{:S(2)}) async-start(), calls=%async_computation.2 | async-start | bytes 2228224 | tf_op jit(solution)/shard_map/reduce_scatter | solution.py:39
  8.7 264.3 %copy-start.1 = (f32[4096]{0:T(1024)S(1)}, f32[4096]{0:T(1024)}, u32[]{:S(2)}) copy-start(f32[4096]{0:T(1024)} %param.9) | copy-start | bytes 49156
  8.7 264.3 %copy-start.2 = (bf16[4096,128]{1,0:T(8,128)(2,1)S(1)}, bf16[4096,128]{1,0:T(8,128)(2,1)}, u32[]{:S(2)}) copy-start(bf16[4096,128]{1,0:T(8,128)(2,1)} %param.7) | copy-start | bytes 3145732
  303.2 129.9 %all-gather.2.cloned.1.call-start = ((), (), s32[]{:S(2)}) async-start(), calls=%async_computation.3 | async-start | bytes 2228224 | tf_op jit(solution)/shard_map/all_gather | solution.py:61
  392.6 101.3 %reduce-scatter.5.cloned.1.call-start = ((), (), s32[]{:S(2)}) async-start(), calls=%async_computation.4 | async-start | bytes 1572864 | tf_op jit(solution)/shard_map/reduce_scatter | solution.py:65
  434.8 59.1 %copy-start.3 = (f32[128]{0:T(128)S(1)}, f32[128]{0:T(128)}, u32[]{:S(2)}) copy-start(f32[128]{0:T(128)} %param.13) | copy-start | bytes 1540
Sparse Core Ops, SparseCore 0:
  303.3 64.5 reduce-scatter.2
  392.7 40.3 all-gather.1
  461.4 19.1 reduce-scatter.4
where the time goes:
time: 506 us; the launch traced here: 505 us
  other arithmetic  267 us (53%)
  waiting for transfers between devices  105 us (21%)
  matrix products  81.5 us (16%)
  blocking collectives  32 us (6%)
  between operations  13.2 us (3%)
  local copies, waits for them, and re-layouts  6.8 us (1%)
    another operation x2, other arithmetic  264 us
    reduce_scatter x1, waiting for transfers between devices, on_device(): lax.psum_scatter(term.reshape(2, lax.axis_size('pts') * own_modes, width)...  64.5 us
    all_gather x1, waiting for transfers between devices, on_device(): piece = lax.all_gather(filtered, 'pts', axis=0, tiled=True)  40.5 us
    psum x1, blocking collectives, on_device(): total = lax.psum(jnp.sum(quad_weight), 'pts')  32 us
    dot_general x1, matrix products, on_device(): lax.dot_general(basis, weighted, (((0,), (0,)), ((), ())), preferred_elem...  27.4 us
    dot_general x1, matrix products, on_device(): field = jnp.dot(basis, rhs, preferred_element_type=jnp.float32)  26.5 us
  transfers between devices with their start and end apart: 3, of which 2 were waited for; matrix products, arithmetic and copies ran while one was open for 0% of the time, Pallas kernels for 0%

commit v1 on v0

--- a/solution.py
+++ b/solution.py
@@ -58,7 +58,8 @@
     filtered = jnp.concatenate([real_out, imag_out], axis=1).astype(jnp.bfloat16)
     out_rows = local_pts // n_groups
     my_features = lax.dynamic_slice_in_dim(features, group * out_rows, out_rows, 0)
-    piece = lax.all_gather(filtered, "pts", axis=0, tiled=True)
+    outgoing = jnp.stack([filtered] * lax.axis_size("pts"))
+    piece = jnp.concatenate(lax.all_to_all(outgoing, "pts", 0, 0), axis=0)
     basis = pick_columns(piece.shape[0])
     rhs = jnp.concatenate([piece[:, :width], piece[:, width:]], axis=0)
     field = jnp.dot(basis, rhs, preferred_element_type=jnp.float32)

time: 506 us -> 516 us (1.020)
  blocking collectives: 32 us -> 84.5 us
  waiting for transfers between devices: 105 us -> 64.5 us
    all_to_all x0 -> x1, blocking collectives: none -> 50.6 us  [on_device(): piece = jnp.concatenate(lax.all_to_all(outgoing, 'pts', 0, 0), axis=0)]
    all_gather x1 -> x0, waiting for transfers between devices: 40.5 us -> none  [on_device(): piece = lax.all_gather(filtered, 'pts', axis=0, tiled=True)]
  transfers between devices with their start and end apart: 3 -> 2, of which waited for: 2 -> 1; matrix products, arithmetic and copies ran while one was open for 0% -> 0% of each run, Pallas kernels for 0% -> 0%
where the time goes in v1:
time: 516 us
  other arithmetic  266 us (52%)
  blocking collectives  84.5 us (16%)
  matrix products  81.6 us (16%)
  waiting for transfers between devices  64.5 us (12%)
  between operations  13.5 us (3%)
  local copies, waits for them, and re-layouts  5.43 us (1%)
    another operation x2, other arithmetic  264 us
    reduce_scatter x1, waiting for transfers between devices, on_device(): lax.psum_scatter(term.reshape(2, lax.axis_size('pts') * own_modes, width)...  64.5 us
    all_to_all x1, blocking collectives, on_device(): piece = jnp.concatenate(lax.all_to_all(outgoing, 'pts', 0, 0), axis=0)  50.6 us
    psum x1, blocking collectives, on_device(): total = lax.psum(jnp.sum(quad_weight), 'pts')  33.9 us
    dot_general x1, matrix products, on_device(): lax.dot_general(basis, weighted, (((0,), (0,)), ((), ())), preferred_elem...  27.4 us
    dot_general x1, matrix products, on_device(): field = jnp.dot(basis, rhs, preferred_element_type=jnp.float32)  26.5 us
  transfers between devices with their start and end apart: 2, of which 1 were waited for; matrix products, arithmetic and copies ran while one was open for 0% of the time, Pallas kernels for 0%

profile of v1, /device:TPU:0, one launch (start us, length us, event | category | flops | bytes accessed | tf_op | source)
XLA Modules:
  0.0 515.6 jit_solution(15989069221392253036)
XLA Ops:
  6.5 0.9 convert_element_type.34
  7.5 0.1 reshape.29
  7.6 1.0 fusion.36
  8.6 0.1 constant_dynamic-slice_fusion.1
  8.7 264.2 %cosine_convert_fusion = (bf16[4096,4096]{1,0:T(8,128)(2,1)}, bf16[4096,4096]{1,0:T(8,128)(2,1)}) fusion(f32[4096]{0:T(1024)S(1)} %bitcast.47, f32[4096]{0:T(1024)S(1)} %bitcast.49, f32[4096]{0:T(1024)S(1)} %bitcast.46, f32[4096]{0:T(1024)S(1)} %bitcast.50, f32[4096]{0:T(1024)S(1)} %bitcast.45, f32[4096]{0:T(1024)S(1)} %bitcast.48), kind=kLoop, calls=%fused_computation.2 | loop fusion | flops 150994944 | bytes 67207168 | tf_op jit(solution)/shard_map/convert.2
  272.9 27.4 %fusion.2 = bf16[8192,128]{1,0:T(8,128)(2,1)S(1)} fusion(bf16[4096,4096]{1,0:T(8,128)(2,1)} %get-tuple-element.10, bf16[4096,4096]{1,0:T(8,128)(2,1)} %get-tuple-element.9, bf16[4096,128]{1,0:T(8,128)(2,1)S(1)} %copy-done.2, f32[4096]{0:T(1024)S(1)} %copy-done.1), kind=kOutput, calls=%fused_computation.6 | convolution fusion | flops 8726773760 | bytes 70270976 | tf_op jit(solution)/shard_map/dot_general | solution.py:36
  300.3 2.8 copy.8
  303.1 0.0 reduce-scatter.3.cloned.1.call-update
  303.1 0.2 reduce-scatter.5.cloned.1.call-start
  303.3 64.5 %reduce-scatter.3.cloned.1.call-done = bf16[256,256]{0,1:T(8,128)(2,1)} async-done(((bf16[4096,256]{0,1:T(8,128)(2,1)}), bf16[256,256]{0,1:T(8,128)(2,1)}) %reduce-scatter.3.cloned.1.call-update) | async-done | bytes 131088 | tf_op jit(solution)/shard_map/reduce_scatter | solution.py:39
  367.8 0.9 slice_bitcast_fusion
  368.7 0.1 copy.9
  368.8 5.7 %fusion.9 = f32[256,1,128]{2,1,0:T(1,128)S(1)} fusion(bf16[256,128,1]{1,2,0:T(2,128)(2,1)S(1)} %copy.9, bf16[256,2,128,128]{3,2,1,0:T(8,128)(2,1)} %param.11), kind=kOutput, calls=%fused_computation.13 | convolution fusion | flops 8388608 | bytes 8585216 | tf_op jit(solution)/shard_map/mc,mcd->md/dot_general | solution.py:52
  374.5 5.7 %fusion.3 = f32[256,1,128]{2,1,0:T(1,128)S(1)} fusion(bf16[256,128,1]{1,2,0:T(2,128)(2,1)S(1)} %copy.9, bf16[256,2,128,128]{3,2,1,0:T(8,128)(2,1)} %param.11), kind=kOutput, calls=%fused_computation.7 | convolution fusion | flops 8388608 | bytes 8585216 | tf_op jit(solution)/shard_map/mc,mcd->md/dot_general | solution.py:55
  380.2 0.1 copy.11
  380.3 5.7 %fusion.5 = f32[256,1,128]{2,1,0:T(1,128)S(1)} fusion(bf16[256,128,1]{1,2,0:T(2,128)(2,1)S(1)} %copy.11, bf16[256,2,128,128]{3,2,1,0:T(8,128)(2,1)} %param.11), kind=kOutput, calls=%fused_computation.9 | convolution fusion | flops 8388608 | bytes 8585216 | tf_op jit(solution)/shard_map/mc,mcd->md/dot_general | solution.py:54
  386.0 5.7 %fusion.7 = f32[256,1,128]{2,1,0:T(1,128)S(1)} fusion(bf16[256,128,1]{1,2,0:T(2,128)(2,1)S(1)} %copy.11, bf16[256,2,128,128]{3,2,1,0:T(8,128)(2,1)} %param.11), kind=kOutput, calls=%fused_computation.11 | convolution fusion | flops 8388608 | bytes 8585216 | tf_op jit(solution)/shard_map/mc,mcd->md/dot_general | solution.py:57
  391.8 0.2 stack.2
  392.0 50.6 %all_to_all.5 = bf16[16,256,256]{2,1,0:T(8,128)(2,1)S(1)} all-to-all(bf16[16,256,256]{2,1,0:T(8,128)(2,1)S(1)} %stack.2), channel_id=1, replica_groups=mesh['pts'=16,'modes'=2] {'pts'}, dimensions={0} | all-to-all | bytes 4194304 | tf_op jit(solution)/shard_map/all_to_all | solution.py:62
  442.6 0.1 fusion.35
  442.8 26.5 %fusion.15 = bf16[4096,128]{1,0:T(8,128)(2,1)} fusion(bf16[4096,4096]{1,0:T(8,128)(2,1)} %get-tuple-element.10, bf16[4096,4096]{1,0:T(8,128)(2,1)} %get-tuple-element.9, bf16[4096,128]{1,0:T(8,128)(2,1)S(1)} %get-tuple-element.6, bf16[4096,128]{1,0:T(8,128)(2,1)S(1)} %get-tuple-element.5), kind=kOutput, calls=%fused_computation.19 | convolution fusion | flops 8728870912 | bytes 70254592 | tf_op jit(solution)/shard_map/dot_general | solution.py:65
  469.3 0.6 reduce_sum.9
  469.9 33.9 %psum.7 = f32[]{:T(128)} all-reduce(f32[]{:T(128)} %reduce_sum.9), channel_id=1, replica_groups=mesh['pts'=16,'modes'=2] {'pts'}, use_global_device_ids=true, to_apply=%region_3.0 | all-reduce | flops 1 | bytes 8 | tf_op jit(solution)/shard_map/psum | solution.py:24
  503.8 5.0 fusion.22
  (13 shorter events, 0.1 us)
Async XLA Ops:
  6.5 497.3 %copy-start = (bf16[128,128]{1,0:T(8,128)(2,1)S(1)}, bf16[128,128]{1,0:T(8,128)(2,1)}, u32[]{:S(2)}) copy-start(bf16[128,128]{1,0:T(8,128)(2,1)} %param.12) | copy-start | bytes 98308
  6.5 361.3 %reduce-scatter.3.cloned.1.call-start = ((), (), s32[]{:S(2)}) async-start(), calls=%async_computation.3 | async-start | bytes 2228224 | tf_op jit(solution)/shard_map/reduce_scatter | solution.py:39
  8.7 264.3 %copy-start.1 = (f32[4096]{0:T(1024)S(1)}, f32[4096]{0:T(1024)}, u32[]{:S(2)}) copy-start(f32[4096]{0:T(1024)} %param.9) | copy-start | bytes 49156
  8.7 264.3 %copy-start.2 = (bf16[4096,128]{1,0:T(8,128)(2,1)S(1)}, bf16[4096,128]{1,0:T(8,128)(2,1)}, u32[]{:S(2)}) copy-start(bf16[4096,128]{1,0:T(8,128)(2,1)} %param.7) | copy-start | bytes 3145732
  303.1 200.7 %reduce-scatter.5.cloned.1.call-start = ((), (), s32[]{:S(2)}) async-start(), calls=%async_computation.4 | async-start | bytes 1572864 | tf_op jit(solution)/shard_map/reduce_scatter | solution.py:66
  442.8 61.1 %copy-start.3 = (f32[128]{0:T(128)S(1)}, f32[128]{0:T(128)}, u32[]{:S(2)}) copy-start(f32[128]{0:T(128)} %param.13) | copy-start | bytes 1540
Sparse Core Ops, SparseCore 0:
  303.2 64.5 reduce-scatter.2
  469.4 20.8 reduce-scatter.4
